TPU v7x, 128 devices: a whole 4x4x4 slice. The times are simulated.
128 devices in a mesh: req: 8 (over y, z_hi), mlp: 16 (over z_lo, x, core).
Axes of the slice: x: 4, y: 4, z: 4 (z_hi: 2, z_lo: 2; z = z_hi * 2 + z_lo), core: 2. Of those that a mesh axis runs over, the one named last changes fastest.
Arguments:
- prompt_tokens: bfloat16 [16, 1024, 2048], P('req', None, 'mlp'), may hold values from -6 to 6
- decode_tokens: bfloat16 [32, 2048], P('req', 'mlp'), may hold values from -6 to 6
- prompt_lengths: int32 [16], P('req'), may hold values from 128 to 1024, as said below
- decode_states: float32 [32, 16, 128, 128], P('req', 'mlp'), may hold values from -6 to 6
- w_fio: float32 [2048, 6144], P('req', 'mlp'), may hold values from -0.125 to 0.125
- forget_bias: float32 [2048], P('mlp'), as said below
- head_gain: float32 [2048], P('mlp'), may hold values from 0.1 to 1.9
- w_out: float32 [2048, 2048], P('mlp', 'req'), may hold values from -0.125 to 0.125
- mlp_gain: float32 [2048], replicated, may hold values from 0.1 to 1.9
- w_gu: float32 [2048, 11264], P('req', 'mlp'), may hold values from -0.125 to 0.125
- w_down: float32 [5632, 2048], P('mlp', 'req'), may hold values from -0.078125 to 0.078125
Outputs:
- prompt_out: bfloat16 [16, 1024, 2048], P('req', None, 'mlp')
- decode_out: bfloat16 [32, 2048], P('req', 'mlp')
- prompt_states: float32 [16, 16, 128, 128], P('req', 'mlp')
- decode_next: float32 [32, 16, 128, 128], P('req', 'mlp')
Inputs may be any that keep to these rules, and one draw needn't show every extreme that they name: `prompt_lengths`: slots at or past a prompt's length are padding; one prompt has length 1024 and another 1024 // 8. `forget_bias`: every entry is at least 3 and at most ln(1024) + 1.7.
All inputs are finite; a program needn't handle non-finite values.
Results may differ from a plain program's by a relative error of at most 0.02.
Values may be sent and summed in bfloat16 or wider, within the bound.
No kernel may reach another device: no remote copies, remote signals or barrier semaphores. Data moves between devices by JAX's collectives and lax.ppermute only.
A program may use at most 128 MiB of HBM per device.

v0:
```python
import jax
import jax.numpy as jnp
from jax import lax
from jax.sharding import PartitionSpec as P

BLOCK = 64
epsilon = 1e-05


def add_columns(operand, weights_piece):
    return jnp.dot(operand, weights_piece, preferred_element_type=jnp.float32)


def project_output(source_rows, weights):
    return jnp.dot(
        source_rows,
        lax.all_gather(weights, "req", axis=1, tiled=True),
        preferred_element_type=jnp.float32,
    )


def block_step(carried, forget_block, value_block, query_block, start_row, lengths):
    steps_here = forget_block.shape[1]
    positions = start_row + jnp.arange(steps_here, dtype=jnp.int32)
    alive_mask = (positions[None, :] < lengths[:, None])[:, :, None, None]
    log_forget = jnp.where(alive_mask, jax.nn.log_sigmoid(forget_block), 0.0)
    key_gate = jnp.where(alive_mask, jax.nn.sigmoid(-forget_block), 0.0)
    cumulated = jnp.cumsum(log_forget, axis=1)
    query_tilde = query_block * jnp.exp(cumulated)
    key_tilde = key_gate * jnp.exp(-cumulated)
    scores = jnp.einsum("pthc,pshc->phts", query_tilde, key_tilde, precision=lax.Precision.HIGHEST)
    triangle = jnp.arange(steps_here)[:, None] >= jnp.arange(steps_here)[None, :]
    scores = jnp.where(triangle, scores, 0.0)
    emitted = jnp.einsum("phts,pshv->pthv", scores, value_block, precision=lax.Precision.HIGHEST)
    emitted = emitted + jnp.einsum(
        "pthc,phcv->pthv", query_tilde, carried, precision=lax.Precision.HIGHEST
    )
    emitted = jnp.where(alive_mask, emitted, 0.0)
    last_log = cumulated[:, -1]
    key_decayed = key_gate * jnp.exp(last_log[:, None] - cumulated)
    carried = jnp.exp(last_log)[..., None] * carried + jnp.einsum(
        "pthc,pthv->phcv", key_decayed, value_block, precision=lax.Precision.HIGHEST
    )
    return (carried, emitted)


def on_device(
    prompt_tokens,
    decode_tokens,
    prompt_lengths,
    decode_states,
    w_fio,
    forget_bias,
    head_gain,
    w_out,
    mlp_gain,
    w_gu,
    w_down,
):
    prompts_here, plen, feature_part = prompt_tokens.shape
    heads_here = decode_states.shape[1]
    head_size = decode_states.shape[2]
    prompt_rows = prompts_here * plen
    local_rows = jnp.concatenate(
        [prompt_tokens.reshape(prompt_rows, feature_part), decode_tokens], axis=0
    )
    row_count = local_rows.shape[0]
    x_full = lax.all_gather(local_rows, "mlp", axis=1, tiled=True)
    model_width = x_full.shape[1]
    mixing = add_columns(
        x_full, lax.all_gather(w_fio.astype(jnp.bfloat16), "req", axis=0, tiled=True)
    )
    mixing = mixing.reshape(row_count, heads_here, 3, head_size)
    bias_table = forget_bias.reshape(heads_here, head_size)
    forget_logit = mixing[:, :, 0] + bias_table
    values = mixing[:, :, 1]
    queries = mixing[:, :, 2]
    prompt_forget = forget_logit[:prompt_rows].reshape(prompts_here, plen, heads_here, head_size)
    prompt_values = values[:prompt_rows].reshape(prompts_here, plen, heads_here, head_size)
    prompt_queries = queries[:prompt_rows].reshape(prompts_here, plen, heads_here, head_size)
    start_state = jnp.zeros((prompts_here, heads_here, head_size, head_size), jnp.float32)
    block_total = plen // BLOCK

    def to_blocks(source_array):
        return source_array.reshape(
            prompts_here, block_total, BLOCK, heads_here, head_size
        ).transpose(1, 0, 2, 3, 4)

    def scan_block(carried, inputs):
        forget_block, value_block, query_block, start_row = inputs
        return block_step(
            carried, forget_block, value_block, query_block, start_row, prompt_lengths
        )

    starts = jnp.arange(block_total, dtype=jnp.int32) * BLOCK
    prompt_states, block_outputs = lax.scan(
        scan_block,
        start_state,
        (to_blocks(prompt_forget), to_blocks(prompt_values), to_blocks(prompt_queries), starts),
    )
    prompt_mixed = block_outputs.transpose(1, 0, 2, 3, 4).reshape(
        prompts_here, plen, heads_here, head_size
    )
    decode_logit = forget_logit[prompt_rows:]
    decode_next = (
        jax.nn.sigmoid(decode_logit)[..., None] * decode_states
        + jax.nn.sigmoid(-decode_logit)[..., None] * values[prompt_rows:][:, :, None, :]
    )
    decode_mixed = jnp.einsum(
        "nhcv,nhc->nhv", decode_next, queries[prompt_rows:], precision=lax.Precision.HIGHEST
    )
    mixed_all = jnp.concatenate(
        [prompt_mixed.reshape(prompt_rows, heads_here, head_size), decode_mixed], axis=0
    )
    mean_square = jnp.mean(mixed_all * mixed_all, axis=-1, keepdims=True)
    head_rows = (
        mixed_all * lax.rsqrt(mean_square + epsilon) * head_gain.reshape(heads_here, head_size)
    ).astype(jnp.bfloat16)
    head_rows = head_rows.reshape(row_count, heads_here * head_size)
    offset = lax.axis_index("mlp") * feature_part
    head_terms = project_output(head_rows, w_out.astype(jnp.bfloat16))
    attention = lax.psum_scatter(
        head_terms.astype(jnp.bfloat16), "mlp", scatter_dimension=1, tiled=True
    ).astype(jnp.float32)
    residual = (local_rows.astype(jnp.float32) + attention).astype(jnp.bfloat16)
    residual_wide = residual.astype(jnp.float32)
    square_sum = lax.psum(jnp.sum(residual_wide * residual_wide, axis=1), "mlp")
    row_scale = lax.rsqrt(square_sum / model_width + epsilon)[:, None]
    gain_part = lax.dynamic_slice_in_dim(mlp_gain, offset, feature_part)
    normed_part = (residual_wide * row_scale * gain_part).astype(jnp.bfloat16)
    normed = lax.all_gather(normed_part, "mlp", axis=1, tiled=True)
    gate_up = add_columns(
        normed, lax.all_gather(w_gu.astype(jnp.bfloat16), "req", axis=0, tiled=True)
    )
    hidden_here = w_gu.shape[1] // 2
    hidden = (jax.nn.silu(gate_up[:, :hidden_here]) * gate_up[:, hidden_here:]).astype(jnp.bfloat16)
    down_terms = jnp.dot(
        hidden,
        lax.all_gather(w_down.astype(jnp.bfloat16), "req", axis=1, tiled=True),
        preferred_element_type=jnp.float32,
    )
    down_share = lax.psum_scatter(
        down_terms.astype(jnp.bfloat16), "mlp", scatter_dimension=1, tiled=True
    ).astype(jnp.float32)
    layer_output = (residual_wide + down_share).astype(jnp.bfloat16)
    prompt_out = layer_output[:prompt_rows].reshape(prompts_here, plen, feature_part)
    decode_out = layer_output[prompt_rows:]
    return (prompt_out, decode_out, prompt_states, decode_next)


def solution(mesh):
    placed = (
        P("req", None, "mlp"),
        P("req", "mlp"),
        P("req"),
        P("req", "mlp", None, None),
        P("req", "mlp"),
        P("mlp"),
        P("mlp"),
        P("mlp", "req"),
        P(),
        P("req", "mlp"),
        P("mlp", "req"),
    )
    return jax.shard_map(
        on_device,
        mesh=mesh,
        in_specs=placed,
        out_specs=(
            P("req", None, "mlp"),
            P("req", "mlp"),
            P("req", "mlp", None, None),
            P("req", "mlp", None, None),
        ),
        check_vma=False,
    )
```

profile of v0, /device:TPU:0, one launch (start us, length us, event | category | flops | bytes accessed | tf_op | source)
XLA Modules:
  0.0 637.0 jit_solution(2306237471951861111)
XLA Ops:
  7.2 1.8 convert_element_type.49
  10.7 38.0 %all_gather.20 = bf16[128,2048]{1,0:T(8,128)(2,1)} all-gather(bf16[128,256]{1,0:T(8,128)(2,1)S(1)} %convert_element_type.51), channel_id=1, replica_groups=mesh['req'=8,'mlp'=16] {'req'}, dimensions={1}, use_global_device_ids=true | all-gather | bytes 589824 | tf_op jit(solution)/shard_map/all_gather | solution.py:17
  48.7 17.3 %all-gather.8.cloned.1.call-done = bf16[2048,384]{1,0:T(8,128)(2,1)} async-done(((bf16[256,384]{1,0:T(8,128)(2,1)}), bf16[2048,384]{1,0:T(8,128)(2,1)}) %all-gather.8.cloned.1.call-update) | async-done | bytes 1572880 | tf_op jit(solution)/shard_map/all_gather | solution.py:71
  66.1 61.3 %all-gather.6.cloned.1.call-done = bf16[2052,2048]{1,0:T(8,128)(2,1)} async-done(((bf16[2052,128]{1,0:T(8,128)(2,1)}), bf16[2052,2048]{1,0:T(8,128)(2,1)}) %all-gather.6.cloned.1.call-update) | async-done | bytes 8405008 | tf_op jit(solution)/shard_map/all_gather | solution.py:68
  127.4 7.4 %fusion.59 = f32[2052,384]{0,1:T(8,128)S(1)} fusion(bf16[2052,2048]{1,0:T(8,128)(2,1)} %all-gather.6.cloned.1.call-done, bf16[2048,384]{1,0:T(8,128)(2,1)} %all-gather.8.cloned.1.call-done), kind=kOutput, calls=%fused_computation.84 | convolution fusion | flops 3227516928 | bytes 13129728 | tf_op jit(solution)/shard_map/dot_general | solution.py:11
  137.3 2.2 copy-done.4
  140.8 2.6 copy.47
  144.7 108.7 %while.13 = (s32[]{:T(128)}, f32[2,1,128,128]{3,2,0,1:T(8,128)S(1)}, f32[16,2,64,1,128]{4,2,0,1,3:T(8,128)}, s32[16]{0:T(128)S(1)}, s32[2]{0:T(128)S(1)}, /*inde...) while((s32[]{:T(128)}, ...), condition=%wide.region_2.3_spmd.clone, body=%wide.region_0.2_spmd.clone.sunk | while | flops 77050048 | bytes 1596940 | solution.py:96
  148.4 1.7 fusion.93
  155.2 1.7 fusion.93
  162.0 1.7 fusion.93
  168.8 1.7 fusion.93
  175.6 1.7 fusion.93
  182.4 1.7 fusion.93
  189.2 1.7 fusion.93
  196.0 1.7 fusion.93
  202.8 1.7 fusion.93
  216.4 1.7 fusion.93
  223.2 1.7 fusion.93
  236.7 1.7 fusion.93
  250.3 1.7 fusion.93
  255.7 5.6 convolution_convert_fusion.1
  261.3 11.6 %copy.58 = bf16[2052,2048]{0,1:T(8,128)(2,1)} copy(bf16[2052,2048]{1,0:T(8,128)(2,1)} %convolution_convert_fusion.1) | data formatting | bytes 16809984
  275.6 73.2 %reduce-scatter.7.cloned.1.call-done = bf16[128,2052]{1,0:T(8,128)(2,1)} async-done(((bf16[2048,2052]{1,0:T(8,128)(2,1)}), bf16[128,2052]{1,0:T(8,128)(2,1)}) %reduce-scatter.7.cloned.1.call-update) | async-done | bytes 525328
  350.5 54.1 %psum.7 = f32[2052]{0:T(1024)S(1)} all-reduce(f32[2052]{0:T(1024)S(1)} %fusion.43), channel_id=1, replica_groups=mesh['req'=8,'mlp'=16] {'mlp'}, use_global_device_ids=true, to_apply=%region_6.7 | all-reduce | flops 2052 | bytes 16416 | tf_op jit(solution)/shard_map/psum | solution.py:127
  406.9 8.9 %all-gather.12.cloned.1.call-done = bf16[2048,704]{0,1:T(8,128)(2,1)} async-done(((bf16[256,704]{0,1:T(8,128)(2,1)}), bf16[2048,704]{0,1:T(8,128)(2,1)}) %all-gather.12.cloned.1.call-update) | async-done | bytes 2883600 | tf_op jit(solution)/shard_map/all_gather | solution.py:133
  415.8 60.6 %all-gather.10.cloned.1.call-done = bf16[2052,2048]{1,0:T(8,128)(2,1)} async-done(((bf16[2052,128]{1,0:T(8,128)(2,1)}), bf16[2052,2048]{1,0:T(8,128)(2,1)}) %all-gather.10.cloned.1.call-update) | async-done | bytes 8405008 | tf_op jit(solution)/shard_map/all_gather | solution.py:131
  476.4 12.6 %fusion.60 = f32[2052,704]{0,1:T(8,128)} fusion(bf16[2052,2048]{1,0:T(8,128)(2,1)} %all-gather.10.cloned.1.call-done, bf16[2048,704]{0,1:T(8,128)(2,1)} %all-gather.12.cloned.1.call-done), kind=kOutput, calls=%fused_computation.85 | convolution fusion | flops 5917114368 | bytes 17067008 | tf_op jit(solution)/shard_map/dot_general | solution.py:11
  489.0 41.2 %all-gather.14.cloned.1.call-done = bf16[352,2048]{1,0:T(8,128)(2,1)} async-done(((bf16[352,256]{1,0:T(8,128)(2,1)}), bf16[352,2048]{1,0:T(8,128)(2,1)}) %all-gather.14.cloned.1.call-update) | async-done | bytes 1441808 | tf_op jit(solution)/shard_map/all_gather | solution.py:139
  530.1 11.1 %convolution_convert_fusion = bf16[2052,2048]{1,0:T(8,128)(2,1)} fusion(bf16[352,2048]{1,0:T(8,128)(2,1)} %all-gather.14.cloned.1.call-done, f32[2052,704]{0,1:T(8,128)} %fusion.60), kind=kOutput, calls=%fused_computation.48 | convolution fusion | flops 2967093504 | bytes 15625216 | tf_op jit(solution)/shard_map/dot_general | solution.py:137
  541.2 11.5 %copy.60 = bf16[2052,2048]{0,1:T(8,128)(2,1)} copy(bf16[2052,2048]{1,0:T(8,128)(2,1)} %convolution_convert_fusion) | data formatting | bytes 16809984
  552.8 74.4 %reduce-scatter.9.cloned.1.call-done = bf16[128,2052]{1,0:T(8,128)(2,1)} async-done(((bf16[2048,2052]{1,0:T(8,128)(2,1)}), bf16[128,2052]{1,0:T(8,128)(2,1)}) %reduce-scatter.9.cloned.1.call-update) | async-done | bytes 525328
  (255 shorter events, 103.6 us)
Async XLA Ops:
  7.2 1.9 copy-start
  7.2 3.5 copy-start.11
  7.2 58.9 %all-gather.8.cloned.1.call-start = ((), (), s32[]{:S(2)}) async-start(), calls=%async_computation.3 | async-start | bytes 1769472 | tf_op jit(solution)/shard_map/all_gather | solution.py:71
  9.0 118.4 %all-gather.6.cloned.1.call-start = ((), (), s32[]{:S(2)}) async-start(), calls=%async_computation.2 | async-start | bytes 8947712 | tf_op jit(solution)/shard_map/all_gather | solution.py:68
  10.6 338.2 %reduce-scatter.7.cloned.1.call-start = ((), (), s32[]{:S(2)}) async-start(), calls=%async_computation.7 | async-start | bytes 9469952
  134.8 1.7 copy-start.3
  136.5 0.7 copy-start.14
  137.2 2.3 copy-start.4
  137.3 3.4 copy-start.1
  143.3 1.3 slice-start
  143.3 1.3 copy-start.15
  144.7 108.8 %copy-start.10 = (f32[4,1,128,128]{3,2,1,0:T(8,128)S(1)}, f32[4,1,128,128]{3,2,1,0:T(8,128)}, u32[]{:S(2)}) copy-start(f32[4,1,128,128]{3,2,1,0:T(8,128)} %param.16) | copy-start | bytes 786436
  253.4 7.9 %copy-start.5 = (f32[2,1,128,128]{3,2,0,1:T(8,128)}, f32[2,1,128,128]{3,2,0,1:T(8,128)S(1)}, u32[]{:S(2)}) copy-start(f32[2,1,128,128]{3,2,0,1:T(8,128)S(1)} %get-tuple-element.114) | copy-start | bytes 393220
  253.4 2.3 copy-start.2
  253.4 2.3 copy-start.6
  253.4 2.3 copy-start.13
  253.6 7.7 %copy-start.7 = (f32[4,1,128,128]{3,2,1,0:T(8,128)}, f32[4,1,128,128]{3,2,1,0:T(8,128)S(1)}, u32[]{:S(2)}) copy-start(f32[4,1,128,128]{3,2,1,0:T(8,128)S(1)} %multiply_add_fusion) | copy-start | bytes 786436
  272.9 1.1 copy-start.8
  272.9 77.2 %copy-start.12 = (bf16[4,128]{1,0:T(4,128)(2,1)S(1)}, bf16[4,128]{1,0:T(4,128)(2,1)}, u32[]{:S(2)}) copy-start(bf16[4,128]{1,0:T(4,128)(2,1)} %param.14) | copy-start | bytes 3076
  272.9 142.9 %all-gather.12.cloned.1.call-start = ((), (), s32[]{:S(2)}) async-start(), calls=%async_computation.5 | async-start | bytes 3244032 | tf_op jit(solution)/shard_map/all_gather | solution.py:133
  274.8 201.6 %all-gather.10.cloned.1.call-start = ((), (), s32[]{:S(2)}) async-start(), calls=%async_computation.4 | async-start | bytes 8947712 | tf_op jit(solution)/shard_map/all_gather | solution.py:131
  350.5 55.4 %copy-start.9 = (f32[352,256]{1,0:T(8,128)S(1)}, f32[352,256]{1,0:T(8,128)}, u32[]{:S(2)}) copy-start(f32[352,256]{1,0:T(8,128)} %param.23) | copy-start | bytes 1081348
  405.9 124.3 %all-gather.14.cloned.1.call-start = ((), (), s32[]{:S(2)}) async-start(), calls=%async_computation.6 | async-start | bytes 1622016 | tf_op jit(solution)/shard_map/all_gather | solution.py:139
  406.7 220.6 %reduce-scatter.9.cloned.1.call-start = ((), (), s32[]{:S(2)}) async-start(), calls=%async_computation.8 | async-start | bytes 9469952
Sparse Core Ops, SparseCore 0:
  10.9 55.1 all-gather.7
  67.7 59.6 all-gather.5
  273.0 75.7 reduce-scatter.6
  351.4 64.3 all-gather.11
  417.3 59.0 all-gather.9
  478.4 51.6 all-gather.13
  552.9 74.2 reduce-scatter.8
where the time goes:
time: 641 us; the launch traced here: 637 us
  waiting for transfers between devices  337 us (53%)
  matrix products  121 us (19%)
  blocking collectives  92.2 us (14%)
  local copies, waits for them, and re-layouts  48.2 us (8%)
  other arithmetic  22.7 us (4%)
  between operations  14.4 us (2%)
    unnamed x9, waiting for transfers between devices  148 us
    all_gather x1, waiting for transfers between devices, on_device(): x_full = lax.all_gather(local_rows, 'mlp', axis=1, tiled=True)  61.3 us
    all_gather x1, waiting for transfers between devices, on_device(): normed = lax.all_gather(normed_part, 'mlp', axis=1, tiled=True)  60.6 us
    psum x1, blocking collectives, on_device(): square_sum = lax.psum(jnp.sum(residual_wide * residual_wide, axis=1), 'mlp')  54.1 us
    all_gather x1, waiting for transfers between devices, on_device(): lax.all_gather(w_down.astype(jnp.bfloat16), 'req', axis=1, tiled=True)  41.2 us
    all_gather x1, blocking collectives, project_output(): lax.all_gather(weights, 'req', axis=1, tiled=True)  38 us
    unnamed x37, local copies, waits for them, and re-layouts  31.3 us
    dot_general x16, matrix products, block_step(): jnp.einsum('pthc,phcv->pthv', query_tilde, carried, precision=lax.Precisi...  27.6 us
  transfers between devices with their start and end apart: 7, of which 7 were waited for; matrix products, arithmetic and copies ran while one was open for 3% of the time, Pallas kernels for 0%

commit v1 on v0

--- a/solution.py
+++ b/solution.py
@@ -65,7 +65,15 @@
         [prompt_tokens.reshape(prompt_rows, feature_part), decode_tokens], axis=0
     )
     row_count = local_rows.shape[0]
-    x_full = lax.all_gather(local_rows, "mlp", axis=1, tiled=True)
+    x_full = jnp.concatenate(
+        lax.all_to_all(
+            jnp.stack(lax.axis_size("mlp") * [local_rows]),
+            axis_name="mlp",
+            split_axis=0,
+            concat_axis=0,
+        ),
+        axis=1,
+    )
     model_width = x_full.shape[1]
     mixing = add_columns(
         x_full, lax.all_gather(w_fio.astype(jnp.bfloat16), "req", axis=0, tiled=True)

time: 641 us -> 672 us (1.048)
  blocking collectives: 92.2 us -> 185 us
  waiting for transfers between devices: 337 us -> 255 us
  local copies, waits for them, and re-layouts: 48.2 us -> 74.6 us
  matrix products: 121 us -> 110 us
    all_gather x1, blocking collectives: 38 us -> 131 us  [project_output(): lax.all_gather(weights, 'req', axis=1, tiled=True)]
    all_gather x1 -> x0, waiting for transfers between devices: 61.3 us -> none  [on_device(): x_full = lax.all_gather(local_rows, 'mlp', axis=1, tiled=True)]
    reshape x0 -> x2, local copies, waits for them, and re-layouts: none -> 27.8 us  [on_device(): jnp.concatenate(lax.all_to_all(jnp.stack(lax.axis_size('mlp') * [local_ro...]
    all_gather x1, waiting for transfers between devices: 17.3 us -> 0.01 us  [on_device(): lax.all_gather(w_fio.astype(jnp.bfloat16), 'req', axis=0, tiled=True)]
    dot_general x16, matrix products: 27.6 us -> 17.5 us  [block_step(): jnp.einsum('pthc,phcv->pthv', query_tilde, carried, precision=lax.Precisi...]
    unnamed x37 -> x28, local copies, waits for them, and re-layouts: 31.3 us -> 27.4 us
    unnamed x9 -> x8, waiting for transfers between devices: 148 us -> 144 us
  transfers between devices with their start and end apart: 7 -> 7, of which waited for: 7 -> 5; matrix products, arithmetic and copies ran while one was open for 3% -> 3% of each run, Pallas kernels for 0% -> 0%
where the time goes in v1:
time: 672 us; the launch traced here: 667 us
  waiting for transfers between devices  255 us (38%)
  blocking collectives  185 us (28%)
  matrix products  110 us (16%)
  local copies, waits for them, and re-layouts  74.6 us (11%)
  other arithmetic  20 us (3%)
  between operations  14.4 us (2%)
    unnamed x8, waiting for transfers between devices  144 us
    all_gather x1, blocking collectives, project_output(): lax.all_gather(weights, 'req', axis=1, tiled=True)  131 us
    all_gather x1, waiting for transfers between devices, on_device(): normed = lax.all_gather(normed_part, 'mlp', axis=1, tiled=True)  60.5 us
    psum x1, blocking collectives, on_device(): square_sum = lax.psum(jnp.sum(residual_wide * residual_wide, axis=1), 'mlp')  54 us
    all_gather x1, waiting for transfers between devices, on_device(): lax.all_gather(w_down.astype(jnp.bfloat16), 'req', axis=1, tiled=True)  41.1 us
    reshape x2, local copies, waits for them, and re-layouts, on_device(): jnp.concatenate(lax.all_to_all(jnp.stack(lax.axis_size('mlp') * [local_ro...  27.8 us
    unnamed x28, local copies, waits for them, and re-layouts  27.4 us
    dot_general x16, matrix products, block_step(): jnp.einsum('pthc,pthv->phcv', key_decayed, value_block, precision=lax.Pre...  21 us
  transfers between devices with their start and end apart: 7, of which 5 were waited for; matrix products, arithmetic and copies ran while one was open for 3% of the time, Pallas kernels for 0%

profile of v1, /device:TPU:0, one launch (start us, length us, event | category | flops | bytes accessed | tf_op | source)
XLA Modules:
  0.0 667.3 jit_solution(323254812539026938)
XLA Ops:
  8.3 4.3 stack.2
  12.6 6.0 all-to-all-start
  19.5 131.1 %all_gather.16 = bf16[128,2048]{1,0:T(8,128)(2,1)S(1)} all-gather(bf16[128,256]{1,0:T(8,128)(2,1)S(1)} %convert_element_type.51), channel_id=1, replica_groups=mesh['req'=8,'mlp'=16] {'req'}, dimensions={1}, use_global_device_ids=true | all-gather | bytes 589824 | tf_op jit(solution)/shard_map/all_gather | solution.py:17
  150.6 1.7 copy.31
  152.4 14.3 %copy.30 = bf16[2052,16,128]{2,1,0:T(8,128)(2,1)} copy(bf16[2052,16,128]{2,0,1:T(8,128)(2,1)} %bitcast.1) | data formatting | bytes 16809984 | tf_op jit(solution)/shard_map/reshape | solution.py:68
  166.7 13.5 %reshape.334 = bf16[2052,2048,1]{1,0,2:T(8,128)(2,1)} reshape(bf16[2052,16,128]{2,1,0:T(8,128)(2,1)} %copy.30) | data formatting | bytes 16809984 | tf_op jit(solution)/shard_map/reshape | solution.py:68
  180.1 7.0 %convolution_bitcast_fusion.2 = f32[2052,1,3,128]{3,0,2,1:T(8,128)S(1)} fusion(bf16[2052,2048,1]{1,0,2:T(8,128)(2,1)} %reshape.334, bf16[3,128,2048]{2,1,0:T(8,128)(2,1)S(1)} %bitcast.183), kind=kOutput, calls=%fused_computation.50 | convolution fusion | flops 3227516928 | bytes 13129728 | tf_op jit(solution)/shard_map/dot_general | solution.py:11
  188.1 1.5 copy_bitcast_fusion
  189.6 98.8 %while.13 = (s32[]{:T(128)}, f32[2,1,128,128]{3,2,0,1:T(8,128)S(1)}, f32[16,2,64,1,128]{4,2,0,1,3:T(8,128)S(1)}, s32[16]{0:T(128)S(1)}, s32[2]{0:T(128)S(1)}, /*...) while((s32[]{:T(128)}, ...), condition=%wide.region_2.3_spmd.clone, body=%wide.region_0.2_spmd.clone.sunk | while | flops 77050048 | bytes 1597324 | solution.py:104
  194.4 1.3 fusion.88
  200.6 1.3 fusion.88
  212.9 1.3 fusion.88
  219.1 1.3 fusion.88
  225.3 1.3 fusion.88
  231.5 1.3 fusion.88
  237.6 1.3 fusion.88
  250.0 1.3 fusion.88
  256.2 1.3 fusion.88
  262.3 1.3 fusion.88
  289.4 5.6 convolution_convert_fusion.1
  295.0 11.6 %copy.39 = bf16[2052,2048]{0,1:T(8,128)(2,1)} copy(bf16[2052,2048]{1,0:T(8,128)(2,1)} %convolution_convert_fusion.1) | data formatting | bytes 16809984
  309.3 69.8 %reduce-scatter.7.cloned.1.call-done = bf16[128,2052]{1,0:T(8,128)(2,1)} async-done(((bf16[2048,2052]{1,0:T(8,128)(2,1)}), bf16[128,2052]{1,0:T(8,128)(2,1)}) %reduce-scatter.7.cloned.1.call-update) | async-done | bytes 525328
  379.1 1.3 copy.40
  380.8 54.0 %psum.7 = f32[2052]{0:T(1024)S(1)} all-reduce(f32[2052]{0:T(1024)S(1)} %fusion.40), channel_id=1, replica_groups=mesh['req'=8,'mlp'=16] {'mlp'}, use_global_device_ids=true, to_apply=%region_6.7 | all-reduce | flops 2052 | bytes 16416 | tf_op jit(solution)/shard_map/psum | solution.py:135
  437.1 9.0 %all-gather.9.cloned.1.call-done = bf16[2048,704]{0,1:T(8,128)(2,1)} async-done(((bf16[256,704]{0,1:T(8,128)(2,1)}), bf16[2048,704]{0,1:T(8,128)(2,1)}) %all-gather.9.cloned.1.call-update) | async-done | bytes 2883600 | tf_op jit(solution)/shard_map/all_gather | solution.py:141
  446.1 60.5 %all-gather.7.cloned.1.call-done = bf16[2052,2048]{1,0:T(8,128)(2,1)} async-done(((bf16[2052,128]{1,0:T(8,128)(2,1)}), bf16[2052,2048]{1,0:T(8,128)(2,1)}) %all-gather.7.cloned.1.call-update) | async-done | bytes 8405008 | tf_op jit(solution)/shard_map/all_gather | solution.py:139
  506.6 12.6 %fusion.57 = f32[2052,704]{0,1:T(8,128)} fusion(bf16[2052,2048]{1,0:T(8,128)(2,1)} %all-gather.7.cloned.1.call-done, bf16[2048,704]{0,1:T(8,128)(2,1)} %all-gather.9.cloned.1.call-done), kind=kOutput, calls=%fused_computation.88 | convolution fusion | flops 5917114368 | bytes 17067008 | tf_op jit(solution)/shard_map/dot_general | solution.py:11
  519.2 41.1 %all-gather.11.cloned.1.call-done = bf16[352,2048]{1,0:T(8,128)(2,1)} async-done(((bf16[352,256]{1,0:T(8,128)(2,1)}), bf16[352,2048]{1,0:T(8,128)(2,1)}) %all-gather.11.cloned.1.call-update) | async-done | bytes 1441808 | tf_op jit(solution)/shard_map/all_gather | solution.py:147
  560.3 11.1 %convolution_convert_fusion = bf16[2052,2048]{1,0:T(8,128)(2,1)} fusion(bf16[352,2048]{1,0:T(8,128)(2,1)} %all-gather.11.cloned.1.call-done, f32[2052,704]{0,1:T(8,128)} %fusion.57), kind=kOutput, calls=%fused_computation.48 | convolution fusion | flops 2967093504 | bytes 15625216 | tf_op jit(solution)/shard_map/dot_general | solution.py:145
  571.4 11.5 %copy.41 = bf16[2052,2048]{0,1:T(8,128)(2,1)} copy(bf16[2052,2048]{1,0:T(8,128)(2,1)} %convolution_convert_fusion) | data formatting | bytes 16809984
  583.0 74.5 %reduce-scatter.9.cloned.1.call-done = bf16[128,2052]{1,0:T(8,128)(2,1)} async-done(((bf16[2048,2052]{1,0:T(8,128)(2,1)}), bf16[128,2052]{1,0:T(8,128)(2,1)}) %reduce-scatter.9.cloned.1.call-update) | async-done | bytes 525328
  657.5 1.3 copy.42
  (245 shorter events, 94.9 us)
Async XLA Ops:
  12.6 6.1 copy-start.4
  12.6 6.9 %copy-start.7 = (f32[128,256]{1,0:T(8,128)S(1)}, f32[128,256]{1,0:T(8,128)}, u32[]{:S(2)}) copy-start(f32[128,256]{1,0:T(8,128)} %param.20) | copy-start | bytes 393220
  12.6 139.8 %all-to-all-start = ((bf16[16,2052,128]{2,1,0:T(8,128)(2,1)}), bf16[16,2052,128]{2,1,0:T(8,128)(2,1)}, u32[]{:S(2)}, u32[]{:S(2)}) async-start(bf16[16,2052,128]{2,1,0:T(8,128)(2,1)} %stack.2), calls=%async_computation | async-start | bytes 16842752 | tf_op jit(solution)/shard_map/all_to_all | solution.py:69
  18.6 132.0 %all-gather.5.cloned.1.call-start = ((), (), s32[]{:S(2)}) async-start(), calls=%async_computation.3 | async-start | bytes 1769472 | tf_op jit(solution)/shard_map/all_gather | solution.py:79
  19.4 359.7 %reduce-scatter.7.cloned.1.call-start = ((), (), s32[]{:S(2)}) async-start(), calls=%async_computation.7 | async-start | bytes 9469952
  187.1 0.7 copy-start.10
  188.1 1.5 copy-start.11
  189.5 98.8 %copy-start.6 = (f32[4,1,128,128]{3,2,1,0:T(8,128)S(1)}, f32[4,1,128,128]{3,2,1,0:T(8,128)}, u32[]{:S(2)}) copy-start(f32[4,1,128,128]{3,2,1,0:T(8,128)} %param.16) | copy-start | bytes 786436
  288.4 6.6 copy-start.1
  288.4 1.0 copy-start.9
  288.6 6.4 copy-start.2
  306.6 1.1 copy-start.3
  306.6 73.8 %copy-start = (bf16[2,1024,128]{2,1,0:T(8,128)(2,1)S(1)}, bf16[2,1024,128]{2,1,0:T(8,128)(2,1)}, u32[]{:S(2)}) copy-start(bf16[2,1024,128]{2,1,0:T(8,128)(2,1)} %param.13) | copy-start | bytes 1572868
  306.7 73.8 %copy-start.8 = (bf16[4,128]{1,0:T(4,128)(2,1)S(1)}, bf16[4,128]{1,0:T(4,128)(2,1)}, u32[]{:S(2)}) copy-start(bf16[4,128]{1,0:T(4,128)(2,1)} %param.14) | copy-start | bytes 3076
  306.7 139.4 %all-gather.9.cloned.1.call-start = ((), (), s32[]{:S(2)}) async-start(), calls=%async_computation.5 | async-start | bytes 3244032 | tf_op jit(solution)/shard_map/all_gather | solution.py:141
  308.5 198.0 %all-gather.7.cloned.1.call-start = ((), (), s32[]{:S(2)}) async-start(), calls=%async_computation.4 | async-start | bytes 8947712 | tf_op jit(solution)/shard_map/all_gather | solution.py:139
  380.5 55.7 %copy-start.5 = (f32[352,256]{1,0:T(8,128)S(1)}, f32[352,256]{1,0:T(8,128)}, u32[]{:S(2)}) copy-start(f32[352,256]{1,0:T(8,128)} %param.23) | copy-start | bytes 1081348
  436.1 124.3 %all-gather.11.cloned.1.call-start = ((), (), s32[]{:S(2)}) async-start(), calls=%async_computation.6 | async-start | bytes 1622016 | tf_op jit(solution)/shard_map/all_gather | solution.py:147
  436.9 220.7 %reduce-scatter.9.cloned.1.call-start = ((), (), s32[]{:S(2)}) async-start(), calls=%async_computation.8 | async-start | bytes 9469952
Sparse Core Ops, SparseCore 0:
  22.3 113.4 all-gather.4
  306.8 72.2 reduce-scatter.6
  381.9 64.1 all-gather.8
  447.5 58.9 all-gather.6
  508.6 51.6 all-gather.10
  583.1 74.3 reduce-scatter.8
